TPU v7x, 32 devices: a whole 2x2x4 slice. The times are simulated.
32 devices in a mesh: expert: 8 (over z, y), replica: 4 (over x, core).
Axes of the slice: x: 2, y: 2, z: 4, core: 2. Of those that a mesh axis runs over, the one named last changes fastest.
Arguments:
- tokens: bfloat16 [4096, 2048], P(('expert', 'replica')), may hold values from -6 to 6
- out_grad: bfloat16 [4096, 2048], P(('expert', 'replica')), may hold values from -6 to 6
- expert_ids: int32 [4096, 2], P(('expert', 'replica')), may hold values from 0 to 3, as said below
- route_weights: bfloat16 [4096, 2], P(('expert', 'replica')), may hold values from 0.25 to 1
- capacity: int32 [4], replicated, may hold values from 2 to 2
- w_gate: bfloat16 [8, 2048, 384], P('expert', 'replica'), may hold values from -0.125 to 0.125
- w_up: bfloat16 [8, 2048, 384], P('expert', 'replica'), may hold values from -0.125 to 0.125
- w_down: bfloat16 [8, 384, 2048], P('expert', None, 'replica'), may hold values from -0.21875 to 0.21875
Outputs:
- x_grad: bfloat16 [4096, 2048], P(('expert', 'replica'))
- gate_grad: bfloat16 [8, 2048, 384], P('expert', 'replica')
- up_grad: bfloat16 [8, 2048, 384], P('expert', 'replica')
- down_grad: bfloat16 [8, 384, 2048], P('expert')
Inputs may be any that keep to these rules, and one draw needn't show every extreme that they name: `expert_ids`: each row names 2 different experts.
All inputs are finite; a program needn't handle non-finite values.
Results may differ from a plain program's by a relative error of at most 0.009.
Values may be sent and summed in bfloat16 or wider, within the bound.
A program may use at most 64 MiB of HBM per device.

v0:
```python
import jax
import jax.numpy as jnp
from jax import lax
from jax.sharding import PartitionSpec as P

CAP = 2


def shards(tokens, out_grad, expert_ids, route_weights, capacity, w_gate, w_up, w_down):
    experts = capacity.shape[0]
    owners = lax.axis_size("expert")
    width = tokens.shape[1]
    slot_count = experts * CAP
    expert_range = jnp.arange(experts, dtype=jnp.int32)
    chosen = (expert_ids[:, :, None] == expert_range[None, None, :]).astype(jnp.int32)
    ranks = jnp.cumsum(jnp.sum(chosen, axis=1), axis=0)
    place = jnp.sum(chosen * ranks[:, None, :], axis=2) - 1
    limit = jnp.sum(chosen * capacity[None, None, :], axis=2)
    slot_ids = jnp.where(place < limit, expert_ids * CAP + place, -1)
    table = slot_ids[None, :, :] == jnp.arange(slot_count, dtype=jnp.int32)[:, None, None]
    picker = jnp.any(table, axis=2).astype(jnp.bfloat16)
    slot_weight = jnp.sum(
        jnp.where(table, route_weights.astype(jnp.float32)[None, :, :], 0.0), axis=(1, 2)
    ).astype(jnp.bfloat16)
    packed = jnp.dot(
        picker, jnp.concatenate([tokens, out_grad], axis=1), preferred_element_type=jnp.float32
    ).astype(jnp.bfloat16)
    packed = packed.reshape(experts, CAP, 2 * width)
    slot_weight = slot_weight.reshape(experts, CAP)
    send_rows = jnp.broadcast_to(packed[:, None], (experts, 2, CAP, 2 * width)).reshape(
        owners, CAP, 2 * width
    )
    send_weight = jnp.broadcast_to(slot_weight[:, None], (experts, 2, CAP)).reshape(owners, CAP)
    got_rows, got_weight = (
        lax.all_to_all(send_rows, "expert", split_axis=0, concat_axis=0, tiled=True),
        lax.all_to_all(send_weight, "expert", split_axis=0, concat_axis=0, tiled=True),
    )
    gate_all, up_all, down_all = (
        lax.all_gather(w_gate, "replica", axis=1, tiled=True),
        lax.all_gather(w_up, "replica", axis=1, tiled=True),
        lax.all_gather(w_down, "replica", axis=2, tiled=True),
    )
    gate_mat = gate_all[0]
    up_mat = up_all[0]
    down_mat = down_all[0]
    row_total = owners * CAP
    flat_rows = got_rows.reshape(row_total, 2 * width)
    inputs = flat_rows[:, :width]
    cotangent = flat_rows[:, width:]
    weights = got_weight.reshape(row_total).astype(jnp.float32)
    gate = jnp.dot(inputs, gate_mat, preferred_element_type=jnp.float32)
    up = jnp.dot(inputs, up_mat, preferred_element_type=jnp.float32)
    sig = jax.nn.sigmoid(gate)
    act = gate * sig
    hidden = (act * up).astype(jnp.bfloat16)
    scaled = (weights[:, None] * cotangent.astype(jnp.float32)).astype(jnp.bfloat16)
    back = lax.dot_general(
        scaled, down_mat, (((1,), (1,)), ((), ())), preferred_element_type=jnp.float32
    )
    gate_back = (back * up * sig * (1.0 + gate * (1.0 - sig))).astype(jnp.bfloat16)
    up_back = (back * act).astype(jnp.bfloat16)
    both_back = jnp.concatenate([gate_back, up_back], axis=1)
    both_mat = jnp.concatenate([gate_mat, up_mat], axis=1)
    partial_value = lax.dot_general(
        both_back, both_mat, (((1,), (1,)), ((), ())), preferred_element_type=jnp.float32
    ).astype(jnp.bfloat16)
    returned = lax.all_to_all(
        partial_value.reshape(owners, CAP, width), "expert", split_axis=0, concat_axis=0, tiled=True
    )
    returned = returned.reshape(experts, 2, CAP, width)
    total = lax.dot_general(
        picker,
        returned[:, 0].reshape(slot_count, width),
        (((0,), (0,)), ((), ())),
        preferred_element_type=jnp.float32,
    )
    total = total + lax.dot_general(
        picker,
        returned[:, 1].reshape(slot_count, width),
        (((0,), (0,)), ((), ())),
        preferred_element_type=jnp.float32,
    )
    x_grad = total.astype(jnp.bfloat16)
    wide_grad = lax.psum_scatter(
        lax.dot_general(
            inputs, both_back, (((0,), (0,)), ((), ())), preferred_element_type=jnp.float32
        )
        .astype(jnp.bfloat16)
        .astype(jnp.bfloat16),
        "replica",
        scatter_dimension=0,
        tiled=True,
    ).astype(jnp.float32)
    half_units = gate_mat.shape[1]
    gate_grad = wide_grad[:, :half_units].astype(jnp.bfloat16)[None]
    up_grad = wide_grad[:, half_units:].astype(jnp.bfloat16)[None]
    down_local = lax.dot_general(
        hidden, scaled, (((0,), (0,)), ((), ())), preferred_element_type=jnp.float32
    )
    down_grad = lax.psum(down_local.astype(jnp.bfloat16), "replica")[None]
    return (x_grad, gate_grad, up_grad, down_grad)


def solution(mesh):
    return jax.shard_map(
        shards,
        mesh=mesh,
        in_specs=(
            P(("expert", "replica"), None),
            P(("expert", "replica"), None),
            P(("expert", "replica"), None),
            P(("expert", "replica"), None),
            P(),
            P("expert", "replica", None),
            P("expert", "replica", None),
            P("expert", None, "replica"),
        ),
        out_specs=(
            P(("expert", "replica"), None),
            P("expert", "replica", None),
            P("expert", "replica", None),
            P("expert", None, None),
        ),
        check_vma=False,
    )
```

profile of v0, /device:TPU:0, one launch (start us, length us, event | category | flops | bytes accessed | tf_op | source)
XLA Modules:
  0.0 171.9 jit_solution(11029008983379027724)
XLA Ops:
  7.2 0.7 all-gather.6.cloned.1.call-update
  7.9 0.7 all-gather.4.cloned.1.call-update
  8.7 0.7 all-gather.8.cloned.1.call-update
  9.4 0.7 convert_reduce_fusion.1
  10.4 0.7 convert_element_type.61
  11.1 0.8 select_reduce_fusion.2
  11.9 0.7 compare_select_fusion
  13.0 0.7 copy.30
  13.7 7.3 %all-to-all-start = ((bf16[8,1,2]{2,1,0:T(2,128)(2,1)}), bf16[8,1,2]{2,1,0:T(2,128)(2,1)S(1)}, u32[]{:S(2)}, u32[]{:S(2)}) async-start(bf16[8,1,2]{2,1,0:T(2,128)(2,1)} %copy.30), calls=%async_computation | async-start | bytes 8192 | tf_op jit(solution)/shard_map/all_to_all | solution.py:36
  21.0 1.4 convolution_convert_fusion
  22.6 4.9 %all-to-all-done = bf16[8,1,2]{2,1,0:T(2,128)(2,1)S(1)} async-done(((bf16[8,1,2]{2,1,0:T(2,128)(2,1)}), bf16[8,1,2]{2,1,0:T(2,128)(2,1)S(1)}, u32[]{:S(2)}, u32[]{:S(2)}) %all-to-all-start) | async-done | bytes 64 | tf_op jit(solution)/shard_map/all_to_all | solution.py:36
  27.5 0.7 broadcast_in_dim.47
  28.2 3.4 %all-to-all-start.1 = ((bf16[8,2,4096]{2,1,0:T(2,128)(2,1)}), bf16[8,2,4096]{2,1,0:T(2,128)(2,1)S(1)}, u32[]{:S(2)}, u32[]{:S(2)}) async-start(bf16[8,2,4096]{2,1,0:T(2,128)(2,1)} %bitcast), calls=%async_computation.1 | async-start | bytes 262144 | tf_op jit(solution)/shard_map/all_to_all | solution.py:35
  31.7 7.1 %all-to-all-done.1 = bf16[8,2,4096]{2,1,0:T(2,128)(2,1)S(1)} async-done(((bf16[8,2,4096]{2,1,0:T(2,128)(2,1)}), bf16[8,2,4096]{2,1,0:T(2,128)(2,1)S(1)}, u32[]{:S(2)}, u32[]{:S(2)}) %all-to-all-start.1) | async-done | bytes 131104 | tf_op jit(solution)/shard_map/all_to_all | solution.py:35
  38.9 1.8 %fusion.17 = f32[16,384]{1,0:T(8,128)S(1)} fusion(bf16[16,4096]{1,0:T(8,128)(2,1)S(1)} %reshape.48, bf16[1,2048,384]{2,1,0:T(8,128)(2,1)} %all-gather.6.cloned.1.call-done), kind=kOutput, calls=%fused_computation.22 | convolution fusion | flops 25165824 | bytes 1662976 | tf_op jit(solution)/shard_map/dot_general | solution.py:52
  40.7 12.4 %all-gather.4.cloned.1.call-done = bf16[1,384,2048]{2,1,0:T(8,128)(2,1)} async-done(((bf16[1,384,512]{2,1,0:T(8,128)(2,1)}), bf16[1,384,2048]{2,1,0:T(8,128)(2,1)}) %all-gather.4.cloned.1.call-update) | async-done | bytes 1572880 | tf_op jit(solution)/shard_map/all_gather | solution.py:41
  53.1 1.9 %fusion.9 = f32[16,384]{1,0:T(8,128)S(1)} fusion(bf16[1,384,2048]{2,1,0:T(8,128)(2,1)} %all-gather.4.cloned.1.call-done, bf16[16,4096]{1,0:T(8,128)(2,1)S(1)} %reshape.48, f32[16]{0:T(128)S(1)} %reshape.51), kind=kOutput, calls=%fused_computation.11 | convolution fusion | flops 25264128 | bytes 1663488 | tf_op jit(solution)/shard_map/dot_general | solution.py:57
  55.1 19.3 %all-gather.8.cloned.1.call-done = bf16[1,2048,384]{2,1,0:T(8,128)(2,1)} async-done(((bf16[1,512,384]{2,1,0:T(8,128)(2,1)}), bf16[1,2048,384]{2,1,0:T(8,128)(2,1)}) %all-gather.8.cloned.1.call-update) | async-done | bytes 1572880 | tf_op jit(solution)/shard_map/all_gather | solution.py:39
  74.4 1.7 %multiply_convert_fusion.3 = (bf16[16,384]{1,0:T(8,128)(2,1)S(1)}, bf16[16,384]{1,0:T(8,128)(2,1)S(1)}, f32[16,384]{1,0:T(8,128)S(1)}) fusion(f32[16,384]{1,0:T(8,128)S(1)} %fusion.9, f32[16,384]{1,0:T(8,128)S(1)} %fusion.17, bf16[1,2048,384]{2,1,0:T(8,128)(2,1)} %all-gather.8.cloned.1.call-done, bf16[16,4096]{1,0:T(8,128)(2,1)S(1)} %reshape.48), kind=kOutput, calls=%fused_computation.27 | convolution fusion | flops 25245696 | bytes 1736704 | tf_op jit(solution)/shard_map/dot_general | solution.py:51
  76.1 2.7 %convolution_convert_fusion.1 = bf16[2048,768]{1,0:T(8,128)(2,1)} fusion(bf16[16,4096]{1,0:T(8,128)(2,1)S(1)} %reshape.48, bf16[16,384]{1,0:T(8,128)(2,1)S(1)} %get-tuple-element.11, bf16[16,384]{1,0:T(8,128)(2,1)S(1)} %get-tuple-element.10), kind=kOutput, calls=%fused_computation.1 | convolution fusion | flops 51953664 | bytes 3235840 | tf_op jit(solution)/shard_map/dot_general | solution.py:85
  78.8 1.4 copy-done
  80.2 0.5 copy-done.1
  80.7 0.9 fusion.6
  81.6 0.7 reshape.49
  82.3 5.5 %all-to-all-start.2 = ((bf16[8,2,2048]{2,1,0:T(2,128)(2,1)}), bf16[8,2,2048]{2,1,0:T(2,128)(2,1)S(1)}, u32[]{:S(2)}, u32[]{:S(2)}) async-start(bf16[8,2,2048]{2,1,0:T(2,128)(2,1)} %reshape.49), calls=%async_computation.2 | async-start | bytes 131072 | tf_op jit(solution)/shard_map/all_to_all | solution.py:67
  87.9 1.8 %fusion.4 = bf16[1,384,2048]{2,1,0:T(8,128)(2,1)} fusion(bf16[16,4096]{1,0:T(8,128)(2,1)S(1)} %reshape.48, f32[16]{0:T(128)S(1)} %reshape.51, f32[16,384]{1,0:T(8,128)S(1)} %fusion.17, f32[16,384]{1,0:T(8,128)S(1)} %get-tuple-element.12), kind=kOutput, calls=%fused_computation.7 | convolution fusion | flops 26087424 | bytes 1688064 | tf_op jit(solution)/shard_map/dot_general | solution.py:97
  89.7 5.1 %all-to-all-done.2 = bf16[8,2,2048]{2,1,0:T(2,128)(2,1)S(1)} async-done(((bf16[8,2,2048]{2,1,0:T(2,128)(2,1)}), bf16[8,2,2048]{2,1,0:T(2,128)(2,1)S(1)}, u32[]{:S(2)}, u32[]{:S(2)}) %all-to-all-start.2) | async-done | bytes 65568 | tf_op jit(solution)/shard_map/all_to_all | solution.py:67
  95.2 1.1 fusion.5
  96.3 20.6 %reduce-scatter.2.cloned.1.call-done = bf16[512,768]{1,0:T(8,128)(2,1)} async-done(((bf16[2048,768]{1,0:T(8,128)(2,1)}), bf16[512,768]{1,0:T(8,128)(2,1)}) %reduce-scatter.2.cloned.1.call-update) | async-done | bytes 786448 | tf_op jit(solution)/shard_map/reduce_scatter | solution.py:84
  116.9 2.1 %slice_bitcast_fusion = (bf16[1,512,384]{2,1,0:T(8,128)(2,1)}, bf16[1,512,384]{2,1,0:T(8,128)(2,1)}) fusion(bf16[512,768]{1,0:T(8,128)(2,1)} %reduce-scatter.2.cloned.1.call-done), kind=kLoop, calls=%fused_computation.16 | loop fusion | bytes 1572864 | tf_op jit(solution)/shard_map/broadcast_in_dim | solution.py:96
  119.0 43.6 %all-reduce.2.cloned.1.call-done = bf16[1,384,2048]{2,1,0:T(8,128)(2,1)} async-done(((bf16[1,384,2048]{2,1,0:T(8,128)(2,1)}), bf16[1,384,2048]{2,1,0:T(8,128)(2,1)}) %all-reduce.2.cloned.1.call-update) | async-done | bytes 1572880 | tf_op jit(solution)/shard_map/psum | solution.py:100
  162.6 2.7 %copy.32 = bf16[1,384,2048]{2,1,0:T(8,128)(2,1)} copy(bf16[1,384,2048]{2,1,0:T(8,128)(2,1)} %all-reduce.2.cloned.1.call-done) | data formatting | bytes 3145728
  (27 shorter events, 1.7 us)
Async XLA Ops:
  7.2 31.8 %all-gather.6.cloned.1.call-start = ((), (), s32[]{:S(2)}) async-start(), calls=%async_computation.5 | async-start | bytes 1966080 | tf_op jit(solution)/shard_map/all_gather | solution.py:40
  7.9 45.2 %all-gather.4.cloned.1.call-start = ((), (), s32[]{:S(2)}) async-start(), calls=%async_computation.4 | async-start | bytes 1966080 | tf_op jit(solution)/shard_map/all_gather | solution.py:41
  8.6 65.7 %all-gather.8.cloned.1.call-start = ((), (), s32[]{:S(2)}) async-start(), calls=%async_computation.6 | async-start | bytes 1966080 | tf_op jit(solution)/shard_map/all_gather | solution.py:39
  13.7 13.7 %all-to-all-start = ((bf16[8,1,2]{2,1,0:T(2,128)(2,1)}), bf16[8,1,2]{2,1,0:T(2,128)(2,1)S(1)}, u32[]{:S(2)}, u32[]{:S(2)}) async-start(bf16[8,1,2]{2,1,0:T(2,128)(2,1)} %copy.30), calls=%async_computation | async-start | bytes 8192 | tf_op jit(solution)/shard_map/all_to_all | solution.py:36
  28.2 10.7 %all-to-all-start.1 = ((bf16[8,2,4096]{2,1,0:T(2,128)(2,1)}), bf16[8,2,4096]{2,1,0:T(2,128)(2,1)S(1)}, u32[]{:S(2)}, u32[]{:S(2)}) async-start(bf16[8,2,4096]{2,1,0:T(2,128)(2,1)} %bitcast), calls=%async_computation.1 | async-start | bytes 262144 | tf_op jit(solution)/shard_map/all_to_all | solution.py:35
  31.6 85.4 %reduce-scatter.2.cloned.1.call-start = ((), (), s32[]{:S(2)}) async-start(), calls=%async_computation.7 | async-start | bytes 3932160 | tf_op jit(solution)/shard_map/reduce_scatter | solution.py:84
  78.8 1.4 copy-start
  78.8 1.9 %copy-start.1 = (bf16[1,2048,384]{2,1,0:T(8,128)(2,1)S(1)}, bf16[1,2048,384]{2,1,0:T(8,128)(2,1)}, u32[]{:S(2)}) copy-start(bf16[1,2048,384]{2,1,0:T(8,128)(2,1)} %all-gather.8.cloned.1.call-done) | copy-start | bytes 4718596
  82.3 12.4 %all-to-all-start.2 = ((bf16[8,2,2048]{2,1,0:T(2,128)(2,1)}), bf16[8,2,2048]{2,1,0:T(2,128)(2,1)S(1)}, u32[]{:S(2)}, u32[]{:S(2)}) async-start(bf16[8,2,2048]{2,1,0:T(2,128)(2,1)} %reshape.49), calls=%async_computation.2 | async-start | bytes 131072 | tf_op jit(solution)/shard_map/all_to_all | solution.py:67
  87.8 74.8 %all-reduce.2.cloned.1.call-start = ((), (), s32[]{:S(2)}) async-start(), calls=%async_computation.8 | async-start | bytes 3145728 | tf_op jit(solution)/shard_map/psum | solution.py:100
Sparse Core Ops, SparseCore 0:
  9.5 22.3 all-gather.5
  33.5 19.6 all-gather.3
  54.7 19.6 all-gather.7
  79.0 37.9 reduce-scatter.1
  119.7 42.8 all-reduce.1
where the time goes:
time: 172 us
  waiting for transfers between devices  115 us (67%)
  starting transfers between devices  16.4 us (10%)
  between operations  13.9 us (8%)
  matrix products  13.7 us (8%)
  local copies, waits for them, and re-layouts  9.59 us (6%)
  other arithmetic  3.13 us (2%)
    psum x1, waiting for transfers between devices, shards(): down_grad = lax.psum(down_local.astype(jnp.bfloat16), 'replica')[None]  43.6 us
    reduce_scatter x1, waiting for transfers between devices, shards(): lax.psum_scatter(lax.dot_general(inputs, both_back, (((0,), (0,)), ((), (...  20.6 us
    all_gather x1, waiting for transfers between devices, shards(): lax.all_gather(w_gate, 'replica', axis=1, tiled=True)  19.3 us
    all_gather x1, waiting for transfers between devices, shards(): lax.all_gather(w_down, 'replica', axis=2, tiled=True)  12.4 us
    all_to_all x1, starting transfers between devices, shards(): lax.all_to_all(send_weight, 'expert', split_axis=0, concat_axis=0, tiled=...  7.31 us
    all_to_all x1, waiting for transfers between devices, shards(): lax.all_to_all(send_rows, 'expert', split_axis=0, concat_axis=0, tiled=True)  7.13 us
    all_to_all x1, starting transfers between devices, shards(): lax.all_to_all(partial_value.reshape(owners, CAP, width), 'expert', split...  5.52 us
    all_to_all x1, waiting for transfers between devices, shards(): lax.all_to_all(partial_value.reshape(owners, CAP, width), 'expert', split...  5.08 us
  transfers between devices with their start and end apart: 8, of which 7 were waited for; matrix products, arithmetic and copies ran while one was open for 10% of the time, Pallas kernels for 0%

commit v1 on v0

--- a/solution.py
+++ b/solution.py
@@ -1,9 +1,23 @@
+import functools
 import jax
 import jax.numpy as jnp
 from jax import lax
 from jax.sharding import PartitionSpec as P
 
 CAP = 2
+
+
+def _attach_cells(target, peer_axis, in_dim):
+    row_list = []
+    for _ in range(lax.axis_size(peer_axis)):
+        row_list.append(target)
+    return jnp.concatenate(
+        lax.all_to_all(jnp.stack(row_list), axis_name=peer_axis, split_axis=0, concat_axis=0),
+        axis=in_dim,
+    )
+
+
+part_notes = functools.partial(_attach_cells, peer_axis="replica", in_dim=1)
 
 
 def shards(tokens, out_grad, expert_ids, route_weights, capacity, w_gate, w_up, w_down):
@@ -36,7 +50,7 @@
         lax.all_to_all(send_weight, "expert", split_axis=0, concat_axis=0, tiled=True),
     )
     gate_all, up_all, down_all = (
-        lax.all_gather(w_gate, "replica", axis=1, tiled=True),
+        part_notes(w_gate),
         lax.all_gather(w_up, "replica", axis=1, tiled=True),
         lax.all_gather(w_down, "replica", axis=2, tiled=True),
     )

time: 172 us -> 163 us (0.948)
  waiting for transfers between devices: 115 us -> 99.3 us
  blocking collectives: 0 us -> 9.74 us
    all_gather x1 -> x0, waiting for transfers between devices: 19.3 us -> none  [shards(): lax.all_gather(w_gate, 'replica', axis=1, tiled=True)]
    all_to_all x0 -> x1, blocking collectives: none -> 9.74 us  [shards(): lax.all_to_all(send_rows, 'expert', split_axis=0, concat_axis=0, tiled=True)]
    all_gather x1, waiting for transfers between devices: 12.4 us -> 17 us  [shards(): lax.all_gather(w_down, 'replica', axis=2, tiled=True)]
    all_to_all x1, starting transfers between devices: 5.52 us -> 3.69 us  [shards(): lax.all_to_all(partial_value.reshape(owners, CAP, width), 'expert', split...]
  transfers between devices with their start and end apart: 8 -> 7, of which waited for: 7 -> 6; matrix products, arithmetic and copies ran while one was open for 10% -> 11% of each run, Pallas kernels for 0% -> 0%
where the time goes in v1:
time: 163 us
  waiting for transfers between devices  99.3 us (61%)
  starting transfers between devices  14.7 us (9%)
  between operations  13.9 us (9%)
  matrix products  12.3 us (8%)
  local copies, waits for them, and re-layouts  9.75 us (6%)
  blocking collectives  9.74 us (6%)
  other arithmetic  3.13 us (2%)
    psum x1, waiting for transfers between devices, shards(): down_grad = lax.psum(down_local.astype(jnp.bfloat16), 'replica')[None]  43.6 us
    reduce_scatter x1, waiting for transfers between devices, shards(): lax.psum_scatter(lax.dot_general(inputs, both_back, (((0,), (0,)), ((), (...  21 us
    all_gather x1, waiting for transfers between devices, shards(): lax.all_gather(w_down, 'replica', axis=2, tiled=True)  17 us
    all_to_all x1, blocking collectives, shards(): lax.all_to_all(send_rows, 'expert', split_axis=0, concat_axis=0, tiled=True)  9.74 us
    all_to_all x1, starting transfers between devices, shards(): lax.all_to_all(send_weight, 'expert', split_axis=0, concat_axis=0, tiled=...  7.31 us
    all_to_all x1, waiting for transfers between devices, _attach_cells(): lax.all_to_all(jnp.stack(row_list), axis_name=peer_axis, split_axis=0, co...  6.2 us
    all_to_all x1, waiting for transfers between devices, shards(): lax.all_to_all(partial_value.reshape(owners, CAP, width), 'expert', split...  5.08 us
    all_to_all x1, waiting for transfers between devices, shards(): lax.all_to_all(send_weight, 'expert', split_axis=0, concat_axis=0, tiled=...  4.89 us
  transfers between devices with their start and end apart: 7, of which 6 were waited for; matrix products, arithmetic and copies ran while one was open for 11% of the time, Pallas kernels for 0%

profile of v1, /device:TPU:0, one launch (start us, length us, event | category | flops | bytes accessed | tf_op | source)
XLA Modules:
  0.0 162.7 jit_solution(8269352875426419456)
XLA Ops:
  7.2 0.7 all-gather.5.cloned.1.call-update
  8.0 0.7 all-gather.3.cloned.1.call-update
  8.7 0.7 convert_reduce_fusion.1
  9.5 0.2 reduce_window_sum.11
  9.7 0.7 convert_element_type.61
  10.4 0.8 select_reduce_fusion.2
  11.1 0.7 compare_select_fusion
  12.3 0.7 copy.30
  13.0 7.3 %all-to-all-start = ((bf16[8,1,2]{2,1,0:T(2,128)(2,1)}), bf16[8,1,2]{2,1,0:T(2,128)(2,1)S(1)}, u32[]{:S(2)}, u32[]{:S(2)}) async-start(bf16[8,1,2]{2,1,0:T(2,128)(2,1)} %copy.30), calls=%async_computation | async-start | bytes 8192 | tf_op jit(solution)/shard_map/all_to_all | solution.py:50
  20.3 1.4 convolution_convert_fusion
  21.8 4.9 %all-to-all-done = bf16[8,1,2]{2,1,0:T(2,128)(2,1)S(1)} async-done(((bf16[8,1,2]{2,1,0:T(2,128)(2,1)}), bf16[8,1,2]{2,1,0:T(2,128)(2,1)S(1)}, u32[]{:S(2)}, u32[]{:S(2)}) %all-to-all-start) | async-done | bytes 64 | tf_op jit(solution)/shard_map/all_to_all | solution.py:50
  26.8 9.7 %all_to_all.24 = bf16[8,2,4096]{2,1,0:T(2,128)(2,1)S(1)} all-to-all(bf16[8,2,4096]{2,1,0:T(2,128)(2,1)S(1)} %bitcast.27), channel_id=1, replica_groups=mesh['expert'=8,'replica'=4] {'expert'}, dimensions={0} | all-to-all | bytes 262144 | tf_op jit(solution)/shard_map/all_to_all | solution.py:49
  36.5 1.3 stack.2
  37.8 3.6 %all-to-all-start.2 = ((bf16[4,1,512,384]{3,2,1,0:T(8,128)(2,1)}), bf16[4,1,512,384]{3,2,1,0:T(8,128)(2,1)S(1)}, u32[]{:S(2)}, u32[]{:S(2)}) async-start(bf16[4,1,512,384]{3,2,1,0:T(8,128)(2,1)} %stack.2), calls=%async_computation.2 | async-start | bytes 3145728 | tf_op jit(solution)/shard_map/all_to_all | solution.py:15
  41.7 1.7 %fusion.17 = f32[16,384]{1,0:T(8,128)S(1)} fusion(bf16[16,4096]{1,0:T(8,128)(2,1)S(1)} %reshape.51, bf16[1,2048,384]{2,1,0:T(8,128)(2,1)} %all-gather.5.cloned.1.call-done), kind=kOutput, calls=%fused_computation.22 | convolution fusion | flops 25165824 | bytes 1662976 | tf_op jit(solution)/shard_map/dot_general | solution.py:66
  43.4 17.0 %all-gather.3.cloned.1.call-done = bf16[1,384,2048]{2,1,0:T(8,128)(2,1)} async-done(((bf16[1,384,512]{2,1,0:T(8,128)(2,1)}), bf16[1,384,2048]{2,1,0:T(8,128)(2,1)}) %all-gather.3.cloned.1.call-update) | async-done | bytes 1572880 | tf_op jit(solution)/shard_map/all_gather | solution.py:55
  60.4 1.9 %fusion.9 = f32[16,384]{1,0:T(8,128)S(1)} fusion(bf16[1,384,2048]{2,1,0:T(8,128)(2,1)} %all-gather.3.cloned.1.call-done, bf16[16,4096]{1,0:T(8,128)(2,1)S(1)} %reshape.51, f32[16]{0:T(128)S(1)} %reshape.54), kind=kOutput, calls=%fused_computation.11 | convolution fusion | flops 25264128 | bytes 1663488 | tf_op jit(solution)/shard_map/dot_general | solution.py:71
  62.3 6.2 %all-to-all-done.2 = bf16[4,1,512,384]{3,2,1,0:T(8,128)(2,1)S(1)} async-done(((bf16[4,1,512,384]{3,2,1,0:T(8,128)(2,1)}), bf16[4,1,512,384]{3,2,1,0:T(8,128)(2,1)S(1)}, u32[]{:S(2)}, u32[]{:S(2)}) %all-to-all-start.2) | async-done | bytes 1572896 | tf_op jit(solution)/shard_map/all_to_all | solution.py:15
  68.5 0.3 multiply_convert_fusion.3
  68.8 2.7 %convolution_convert_fusion.1 = bf16[2048,768]{1,0:T(8,128)(2,1)} fusion(bf16[16,4096]{1,0:T(8,128)(2,1)S(1)} %reshape.51, bf16[16,384]{1,0:T(8,128)(2,1)S(1)} %get-tuple-element.11, bf16[16,384]{1,0:T(8,128)(2,1)S(1)} %get-tuple-element.10), kind=kOutput, calls=%fused_computation.1 | convolution fusion | flops 51953664 | bytes 3235840 | tf_op jit(solution)/shard_map/dot_general | solution.py:99
  71.6 1.4 copy-done
  73.0 0.9 fusion.6
  73.9 0.7 reshape.52
  74.6 3.7 %all-to-all-start.3 = ((bf16[8,2,2048]{2,1,0:T(2,128)(2,1)}), bf16[8,2,2048]{2,1,0:T(2,128)(2,1)S(1)}, u32[]{:S(2)}, u32[]{:S(2)}) async-start(bf16[8,2,2048]{2,1,0:T(2,128)(2,1)} %reshape.52), calls=%async_computation.3 | async-start | bytes 131072 | tf_op jit(solution)/shard_map/all_to_all | solution.py:81
  78.3 1.8 %fusion.4 = bf16[1,384,2048]{2,1,0:T(8,128)(2,1)} fusion(bf16[16,4096]{1,0:T(8,128)(2,1)S(1)} %reshape.51, f32[16]{0:T(128)S(1)} %reshape.54, f32[16,384]{1,0:T(8,128)S(1)} %fusion.17, f32[16,384]{1,0:T(8,128)S(1)} %get-tuple-element.12), kind=kOutput, calls=%fused_computation.7 | convolution fusion | flops 26087424 | bytes 1688064 | tf_op jit(solution)/shard_map/dot_general | solution.py:111
  80.1 5.1 %all-to-all-done.3 = bf16[8,2,2048]{2,1,0:T(2,128)(2,1)S(1)} async-done(((bf16[8,2,2048]{2,1,0:T(2,128)(2,1)}), bf16[8,2,2048]{2,1,0:T(2,128)(2,1)S(1)}, u32[]{:S(2)}, u32[]{:S(2)}) %all-to-all-start.3) | async-done | bytes 65568 | tf_op jit(solution)/shard_map/all_to_all | solution.py:81
  85.3 0.3 fusion.28
  85.6 1.1 fusion.5
  86.8 21.0 %reduce-scatter.2.cloned.1.call-done = bf16[512,768]{1,0:T(8,128)(2,1)} async-done(((bf16[2048,768]{1,0:T(8,128)(2,1)}), bf16[512,768]{1,0:T(8,128)(2,1)}) %reduce-scatter.2.cloned.1.call-update) | async-done | bytes 786448 | tf_op jit(solution)/shard_map/reduce_scatter | solution.py:98
  107.8 2.1 %slice_bitcast_fusion = (bf16[1,512,384]{2,1,0:T(8,128)(2,1)}, bf16[1,512,384]{2,1,0:T(8,128)(2,1)}) fusion(bf16[512,768]{1,0:T(8,128)(2,1)} %reduce-scatter.2.cloned.1.call-done), kind=kLoop, calls=%fused_computation.16 | loop fusion | bytes 1572864 | tf_op jit(solution)/shard_map/broadcast_in_dim | solution.py:110
  109.8 43.6 %all-reduce.2.cloned.1.call-done = bf16[1,384,2048]{2,1,0:T(8,128)(2,1)} async-done(((bf16[1,384,2048]{2,1,0:T(8,128)(2,1)}), bf16[1,384,2048]{2,1,0:T(8,128)(2,1)}) %all-reduce.2.cloned.1.call-update) | async-done | bytes 1572880 | tf_op jit(solution)/shard_map/psum | solution.py:114
  153.5 2.7 %copy.32 = bf16[1,384,2048]{2,1,0:T(8,128)(2,1)} copy(bf16[1,384,2048]{2,1,0:T(8,128)(2,1)} %all-reduce.2.cloned.1.call-done) | data formatting | bytes 3145728
  (26 shorter events, 1.2 us)
Async XLA Ops:
  7.2 29.4 %copy-start.1 = (bf16[1,512,384]{2,1,0:T(8,128)(2,1)S(1)}, bf16[1,512,384]{2,1,0:T(8,128)(2,1)}, u32[]{:S(2)}) copy-start(bf16[1,512,384]{2,1,0:T(8,128)(2,1)} %param.13) | copy-start | bytes 1179652
  7.2 34.5 %all-gather.5.cloned.1.call-start = ((), (), s32[]{:S(2)}) async-start(), calls=%async_computation.6 | async-start | bytes 1966080 | tf_op jit(solution)/shard_map/all_gather | solution.py:54
  7.9 52.5 %all-gather.3.cloned.1.call-start = ((), (), s32[]{:S(2)}) async-start(), calls=%async_computation.5 | async-start | bytes 1966080 | tf_op jit(solution)/shard_map/all_gather | solution.py:55
  13.0 13.7 %all-to-all-start = ((bf16[8,1,2]{2,1,0:T(2,128)(2,1)}), bf16[8,1,2]{2,1,0:T(2,128)(2,1)S(1)}, u32[]{:S(2)}, u32[]{:S(2)}) async-start(bf16[8,1,2]{2,1,0:T(2,128)(2,1)} %copy.30), calls=%async_computation | async-start | bytes 8192 | tf_op jit(solution)/shard_map/all_to_all | solution.py:50
  37.8 30.7 %all-to-all-start.2 = ((bf16[4,1,512,384]{3,2,1,0:T(8,128)(2,1)}), bf16[4,1,512,384]{3,2,1,0:T(8,128)(2,1)S(1)}, u32[]{:S(2)}, u32[]{:S(2)}) async-start(bf16[4,1,512,384]{3,2,1,0:T(8,128)(2,1)} %stack.2), calls=%async_computation.2 | async-start | bytes 3145728 | tf_op jit(solution)/shard_map/all_to_all | solution.py:15
  41.4 66.3 %reduce-scatter.2.cloned.1.call-start = ((), (), s32[]{:S(2)}) async-start(), calls=%async_computation.7 | async-start | bytes 3932160 | tf_op jit(solution)/shard_map/reduce_scatter | solution.py:98
  71.5 1.4 copy-start
  74.6 10.6 %all-to-all-start.3 = ((bf16[8,2,2048]{2,1,0:T(2,128)(2,1)}), bf16[8,2,2048]{2,1,0:T(2,128)(2,1)S(1)}, u32[]{:S(2)}, u32[]{:S(2)}) async-start(bf16[8,2,2048]{2,1,0:T(2,128)(2,1)} %reshape.52), calls=%async_computation.3 | async-start | bytes 131072 | tf_op jit(solution)/shard_map/all_to_all | solution.py:81
  78.3 75.2 %all-reduce.2.cloned.1.call-start = ((), (), s32[]{:S(2)}) async-start(), calls=%async_computation.8 | async-start | bytes 3145728 | tf_op jit(solution)/shard_map/psum | solution.py:114
Sparse Core Ops, SparseCore 0:
  9.5 22.3 all-gather.4
  33.5 26.8 all-gather.2
  71.7 36.0 reduce-scatter.1
  110.6 42.8 all-reduce.1
